TPU v7x, 256 devices: a whole 4x4x8 slice. The times are simulated.
256 devices in a mesh: section: 4 (over x), shard: 64 (over z, y, core).
Axes of the slice: x: 4, y: 4, z: 8, core: 2. Of those that a mesh axis runs over, the one named last changes fastest.
Arguments:
- features: bfloat16 [4096, 768], P('shard'), may hold values from -6 to 6
- tile_cols: int32 [4, 32, 16], P('section'), may hold values from 0 to 31
- live_tiles: int32 [4, 32], P('section'), may hold values from 1 to 16, 256 in all within a row
- tile_values: bfloat16 [4, 4096, 16, 128], P('section', 'shard'), may hold values from -0.375 to 0.375
- degrees: int32 [4, 4096], P('section', 'shard'), may hold values from 1 to 8
Outputs:
- hops: bfloat16 [4, 4096, 768], P('section', 'shard')
Inputs may be any that keep to these rules, and one draw needn't show every extreme that they name: `live_tiles`: every row block has at least one live tile slot; the live counts of one relation sum to 256.
All inputs are finite; a program needn't handle non-finite values.
Results may differ from a plain program's by a relative error of at most 0.0056.
Values may be sent and summed in bfloat16 or wider, within the bound.
A program may use at most 64 MiB of HBM per device.

v0:
```python
import jax
import jax.numpy as jnp
from jax import lax
from jax.sharding import PartitionSpec as P


def from_behind(value, axis, by):
    peers = lax.axis_size(axis)
    pairs = [(i, i + by) for i in range(peers) if 0 <= i + by < peers]
    return lax.ppermute(value, axis, pairs)


def propagate(gathered, block_ids, live_count, tile_rows, row_scale):
    tile_size = tile_rows.shape[2]
    width = gathered.shape[1]
    blocks = gathered.reshape(gathered.shape[0] // tile_size, tile_size, width)
    source = blocks[block_ids]
    live_mask = (jnp.arange(tile_rows.shape[1], dtype=jnp.int32) < live_count).astype(jnp.bfloat16)
    masked = tile_rows * live_mask[None, :, None]
    summed = jnp.einsum("rkc,kcw->rw", masked, source, preferred_element_type=jnp.float32)
    return (summed * row_scale[:, None]).astype(jnp.bfloat16)


def per_device(features, tile_cols, live_tiles, tile_values, degrees):
    section_index = lax.axis_index("section")
    section_count = lax.axis_size("section")
    tile_rows = tile_values[0]
    row_count = tile_rows.shape[0]
    tile_size = tile_rows.shape[2]
    block_row = lax.axis_index("shard") * row_count // tile_size
    block_ids = lax.dynamic_index_in_dim(tile_cols[0], block_row, 0, keepdims=False)
    live_count = lax.dynamic_index_in_dim(live_tiles[0], block_row, 0, keepdims=False)
    row_scale = lax.rsqrt(degrees[0].astype(jnp.float32))
    width = features.shape[1]
    result = jnp.zeros((row_count, width), jnp.bfloat16)
    arrived = jnp.zeros((row_count, width), jnp.bfloat16)
    for hop_num in range(section_count):
        slab_in = jnp.where(section_index == 0, features, arrived)
        gathered = lax.all_gather(slab_in, "shard", axis=0, tiled=True)
        output = propagate(gathered, block_ids, live_count, tile_rows, row_scale)
        result = jnp.where(section_index == hop_num, output, result)
        arrived = from_behind(output, "section", 1)
    return result[None]


def solution(mesh):
    in_specs = (
        P("shard", None),
        P("section", None, None),
        P("section", None),
        P("section", "shard", None, None),
        P("section", "shard"),
    )
    out_specs = P("section", "shard", None)
    return jax.shard_map(
        per_device, mesh=mesh, in_specs=in_specs, out_specs=out_specs, check_vma=False
    )
```

profile of v0, /device:TPU:3, one launch (start us, length us, event | category | flops | bytes accessed | tf_op | source)
XLA Modules:
  0.0 375.5 jit_solution(7608889095608387722)
XLA Ops:
  6.5 0.7 broadcast_select_fusion.3
  7.3 1.3 constant_dynamic-slice_fusion
  9.5 0.7 rsqrt_bitcast_fusion
  10.1 1.0 bitcast_multiply_fusion
  11.2 82.9 %all-gather.5.cloned.1.call-done = bf16[4096,768]{1,0:T(8,128)(2,1)} async-done(((bf16[64,768]{1,0:T(8,128)(2,1)}), bf16[4096,768]{1,0:T(8,128)(2,1)}) %all-gather.5.cloned.1.call-update) | async-done | bytes 6291472 | tf_op jit(solution)/shard_map/all_gather | solution.py:39
  94.0 3.5 gather_fusion
  97.6 0.7 fusion.4
  98.9 3.1 collective-permute-start
  102.0 2.9 collective-permute-done
  104.9 0.7 broadcast_select_fusion.2
  105.6 78.2 %all-gather.7.cloned.1.call-done = bf16[4096,768]{1,0:T(8,128)(2,1)} async-done(((bf16[64,768]{1,0:T(8,128)(2,1)}), bf16[4096,768]{1,0:T(8,128)(2,1)}) %all-gather.7.cloned.1.call-update) | async-done | bytes 6291472 | tf_op jit(solution)/shard_map/all_gather | solution.py:39
  183.8 3.5 gather_fusion.1
  187.3 0.7 fusion.5
  188.6 3.1 collective-permute-start.1
  191.7 2.9 collective-permute-done.1
  194.6 0.7 broadcast_select_fusion.1
  195.3 78.2 %all-gather.9.cloned.1.call-done = bf16[4096,768]{1,0:T(8,128)(2,1)} async-done(((bf16[64,768]{1,0:T(8,128)(2,1)}), bf16[4096,768]{1,0:T(8,128)(2,1)}) %all-gather.9.cloned.1.call-update) | async-done | bytes 6291472 | tf_op jit(solution)/shard_map/all_gather | solution.py:39
  273.5 3.5 gather_fusion.2
  277.0 0.7 fusion.6
  278.3 3.1 collective-permute-start.2
  281.4 2.9 collective-permute-done.2
  285.0 78.2 %all-gather.11.cloned.1.call-done = bf16[4096,768]{1,0:T(8,128)(2,1)} async-done(((bf16[64,768]{1,0:T(8,128)(2,1)}), bf16[4096,768]{1,0:T(8,128)(2,1)}) %all-gather.11.cloned.1.call-update) | async-done | bytes 6291472 | tf_op jit(solution)/shard_map/all_gather | solution.py:39
  363.2 3.6 gather_fusion.3
  366.7 2.2 fusion.9
  (25 shorter events, 3.7 us)
Async XLA Ops:
  6.5 2.1 copy-start
  6.5 87.5 %all-gather.5.cloned.1.call-start = ((), (), s32[]{:S(2)}) async-start(), calls=%async_computation | async-start | bytes 6389760 | tf_op jit(solution)/shard_map/all_gather | solution.py:39
  7.3 176.5 %all-gather.7.cloned.1.call-start = ((), (), s32[]{:S(2)}) async-start(), calls=%async_computation.1 | async-start | bytes 6389760 | tf_op jit(solution)/shard_map/all_gather | solution.py:39
  97.6 7.3 %copy-start.1 = (bf16[64,768]{1,0:T(8,128)(2,1)S(1)}, bf16[64,768]{1,0:T(8,128)(2,1)}, u32[]{:S(2)}) copy-start(bf16[64,768]{1,0:T(8,128)(2,1)} %param.5) | copy-start | bytes 294916
  98.3 0.6 copy-start.2
  98.9 6.0 %collective-permute-start = (bf16[64,768]{1,0:T(8,128)(2,1)S(1)}, bf16[64,768]{1,0:T(8,128)(2,1)S(1)}, u32[]{:S(2)}, u32[]{:S(2)}) collective-permute-start(bf16[64,768]{1,0:T(8,128)(2,1)S(1)} %fusion.4), channel_id=1, source_target_pairs={{0,64},{64,128},{128,192},{1,65},{65,129},{129,193},{2,66},{66,130... | collective-permute-start | bytes 294920 | tf_op jit(solution)/shard_map/ppermute | solution.py:10
  105.5 167.9 %all-gather.9.cloned.1.call-start = ((), (), s32[]{:S(2)}) async-start(), calls=%async_computation.2 | async-start | bytes 6389760 | tf_op jit(solution)/shard_map/all_gather | solution.py:39
  188.0 0.6 copy-start.4
  188.6 6.0 %collective-permute-start.1 = (bf16[64,768]{1,0:T(8,128)(2,1)S(1)}, bf16[64,768]{1,0:T(8,128)(2,1)S(1)}, u32[]{:S(2)}, u32[]{:S(2)}) collective-permute-start(bf16[64,768]{1,0:T(8,128)(2,1)S(1)} %fusion.5), channel_id=1, source_target_pairs={{0,64},{64,128},{128,192},{1,65},{65,129},{129,193},{2,66},{66,130... | collective-permute-start | bytes 294920 | tf_op jit(solution)/shard_map/ppermute | solution.py:10
  195.2 167.9 %all-gather.11.cloned.1.call-start = ((), (), s32[]{:S(2)}) async-start(), calls=%async_computation.3 | async-start | bytes 6389760 | tf_op jit(solution)/shard_map/all_gather | solution.py:39
  277.7 0.6 copy-start.5
  278.3 6.0 %collective-permute-start.2 = (bf16[64,768]{1,0:T(8,128)(2,1)S(1)}, bf16[64,768]{1,0:T(8,128)(2,1)S(1)}, u32[]{:S(2)}, u32[]{:S(2)}) collective-permute-start(bf16[64,768]{1,0:T(8,128)(2,1)S(1)} %fusion.6), channel_id=1, source_target_pairs={{0,64},{64,128},{128,192},{1,65},{65,129},{129,193},{2,66},{66,130... | collective-permute-start | bytes 294920 | tf_op jit(solution)/shard_map/ppermute | solution.py:10
  363.2 3.6 copy-start.3
Sparse Core Ops, SparseCore 0:
  10.1 83.9 all-gather.4
  105.7 78.0 all-gather.6
  195.4 78.0 all-gather.8
  285.1 78.0 all-gather.10
where the time goes:
time: 376 us; the launch traced here: 375 us
  waiting for transfers between devices  326 us (87%)
  local copies, waits for them, and re-layouts  17.5 us (5%)
  between operations  13.3 us (4%)
  starting transfers between devices  9.37 us (2%)
  other arithmetic  4.97 us (1%)
  matrix products  4.2 us (1%)
    all_gather x4, waiting for transfers between devices, per_device(): gathered = lax.all_gather(slab_in, 'shard', axis=0, tiled=True)  317 us
    gather x4, local copies, waits for them, and re-layouts, propagate(): source = blocks[block_ids]  14.2 us
    ppermute x3, starting transfers between devices, from_behind(): return lax.ppermute(value, axis, pairs)  9.25 us
    ppermute x3, waiting for transfers between devices, from_behind(): return lax.ppermute(value, axis, pairs)  8.62 us
  transfers between devices with their start and end apart: 7, of which 7 were waited for; matrix products, arithmetic and copies ran while one was open for 1% of the time, Pallas kernels for 0%

commit v1 on v0

--- a/solution.py
+++ b/solution.py
@@ -36,7 +36,9 @@
     arrived = jnp.zeros((row_count, width), jnp.bfloat16)
     for hop_num in range(section_count):
         slab_in = jnp.where(section_index == 0, features, arrived)
-        gathered = lax.all_gather(slab_in, "shard", axis=0, tiled=True)
+        gathered = jnp.concatenate(
+            lax.all_to_all(jnp.stack([slab_in] * lax.axis_size("shard")), "shard", 0, 0), axis=0
+        )
         output = propagate(gathered, block_ids, live_count, tile_rows, row_scale)
         result = jnp.where(section_index == hop_num, output, result)
         arrived = from_behind(output, "section", 1)

time: 376 us -> 641 us (1.70)
  blocking collectives: 0 us -> 296 us
  waiting for transfers between devices: 326 us -> 283 us
  starting transfers between devices: 9.37 us -> 30.3 us
  between operations: 13.3 us -> 0.23 us
    all_gather x4 -> x0, waiting for transfers between devices: 317 us -> none  [per_device(): gathered = lax.all_gather(slab_in, 'shard', axis=0, tiled=True)]
    all_to_all x0 -> x2, blocking collectives: none -> 296 us  [per_device(): lax.all_to_all(jnp.stack([slab_in] * lax.axis_size('shard')), 'shard', 0, 0)]
    all_to_all x0 -> x2, waiting for transfers between devices: none -> 276 us  [per_device(): lax.all_to_all(jnp.stack([slab_in] * lax.axis_size('shard')), 'shard', 0, 0)]
    all_to_all x0 -> x2, starting transfers between devices: none -> 20.9 us  [per_device(): lax.all_to_all(jnp.stack([slab_in] * lax.axis_size('shard')), 'shard', 0, 0)]
    another operation x0 -> x4, local copies, waits for them, and re-layouts: none -> 8.31 us  [per_device(): jnp.stack([slab_in] * lax.axis_size('shard'))]
  transfers between devices with their start and end apart: 7 -> 5, of which waited for: 7 -> 5; matrix products, arithmetic and copies ran while one was open for 1% -> 0% of each run, Pallas kernels for 0% -> 0%
where the time goes in v1:
time: 641 us; the launch traced here: 638 us
  blocking collectives  296 us (46%)
  waiting for transfers between devices  283 us (44%)
  starting transfers between devices  30.3 us (5%)
  local copies, waits for them, and re-layouts  23.9 us (4%)
    all_to_all x2, blocking collectives, per_device(): lax.all_to_all(jnp.stack([slab_in] * lax.axis_size('shard')), 'shard', 0, 0)  296 us
    all_to_all x2, waiting for transfers between devices, per_device(): lax.all_to_all(jnp.stack([slab_in] * lax.axis_size('shard')), 'shard', 0, 0)  276 us
    all_to_all x2, starting transfers between devices, per_device(): lax.all_to_all(jnp.stack([slab_in] * lax.axis_size('shard')), 'shard', 0, 0)  20.9 us
    gather x4, local copies, waits for them, and re-layouts, propagate(): source = blocks[block_ids]  14.2 us
  transfers between devices with their start and end apart: 5, of which 5 were waited for; matrix products, arithmetic and copies ran while one was open for 0% of the time, Pallas kernels for 0%

profile of v1, /device:TPU:3, one launch (start us, length us, event | category | flops | bytes accessed | tf_op | source)
XLA Modules:
  0.0 638.4 jit_solution(2035338817429019670)
XLA Ops:
  0.0 3.4 stack.8
  3.4 12.6 %all-to-all-start = ((bf16[64,64,768]{2,1,0:T(8,128)(2,1)}), bf16[64,64,768]{2,1,0:T(8,128)(2,1)}, u32[]{:S(2)}, u32[]{:S(2)}) async-start(bf16[64,64,768]{2,1,0:T(8,128)(2,1)} %stack.8), calls=%async_computation | async-start | bytes 12582912 | tf_op jit(solution)/shard_map/all_to_all | solution.py:40
  17.7 137.3 %all-to-all-done = bf16[64,64,768]{2,1,0:T(8,128)(2,1)} async-done(((bf16[64,64,768]{2,1,0:T(8,128)(2,1)}), bf16[64,64,768]{2,1,0:T(8,128)(2,1)}, u32[]{:S(2)}, u32[]{:S(2)}) %all-to-all-start) | async-done | bytes 6291488 | tf_op jit(solution)/shard_map/all_to_all | solution.py:40
  154.9 3.5 gather_fusion
  158.5 0.7 fusion.4
  159.1 3.1 collective-permute-start
  162.3 2.2 collective-permute-done
  164.5 0.8 stack.9
  165.3 148.6 %all_to_all.20 = bf16[64,64,768]{2,1,0:T(8,128)(2,1)} all-to-all(bf16[64,64,768]{2,1,0:T(8,128)(2,1)S(1)} %stack.9), channel_id=1, replica_groups=mesh['section'=4,'shard'=64] {'shard'}, dimensions={0} | all-to-all | bytes 12582912 | tf_op jit(solution)/shard_map/all_to_all | solution.py:40
  313.9 3.5 gather_fusion.1
  317.4 0.7 fusion.5
  318.1 3.1 collective-permute-start.1
  321.2 2.2 collective-permute-done.1
  323.5 0.8 stack.10
  324.2 147.6 %all_to_all.21 = bf16[64,64,768]{2,1,0:T(8,128)(2,1)} all-to-all(bf16[64,64,768]{2,1,0:T(8,128)(2,1)S(1)} %stack.10), channel_id=1, replica_groups=mesh['section'=4,'shard'=64] {'shard'}, dimensions={0} | all-to-all | bytes 12582912 | tf_op jit(solution)/shard_map/all_to_all | solution.py:40
  471.8 3.5 gather_fusion.2
  475.4 0.7 fusion.6
  476.7 3.1 collective-permute-start.2
  479.8 2.2 collective-permute-done.2
  482.0 3.4 stack.11
  485.4 8.3 %all-to-all-start.3 = ((bf16[64,64,768]{2,1,0:T(8,128)(2,1)}), bf16[64,64,768]{2,1,0:T(8,128)(2,1)}, u32[]{:S(2)}, u32[]{:S(2)}) async-start(bf16[64,64,768]{2,1,0:T(8,128)(2,1)} %stack.11), calls=%async_computation.3 | async-start | bytes 12582912 | tf_op jit(solution)/shard_map/all_to_all | solution.py:40
  493.7 138.9 %all-to-all-done.3 = bf16[64,64,768]{2,1,0:T(8,128)(2,1)} async-done(((bf16[64,64,768]{2,1,0:T(8,128)(2,1)}), bf16[64,64,768]{2,1,0:T(8,128)(2,1)}, u32[]{:S(2)}, u32[]{:S(2)}) %all-to-all-start.3) | async-done | bytes 6291488 | tf_op jit(solution)/shard_map/all_to_all | solution.py:40
  632.6 3.6 gather_fusion.3
  636.2 2.2 fusion.9
  (29 shorter events, 2.3 us)
Async XLA Ops:
  0.0 16.7 %copy-start = (s32[1,32,16]{1,2,0:T(8,128)S(1)}, s32[1,32,16]{1,2,0:T(8,128)}, u32[]{:S(2)}) copy-start(s32[1,32,16]{1,2,0:T(8,128)} %param.6) | copy-start | bytes 6148
  3.4 12.7 %copy-start.7 = (s32[1,32]{1,0:T(1,128)S(1)}, s32[1,32]{1,0:T(1,128)}, u32[]{:S(2)}) copy-start(s32[1,32]{1,0:T(1,128)} %param.7) | copy-start | bytes 388
  3.4 14.1 %copy-start.8 = (s32[1,64]{1,0:T(1,128)S(1)}, s32[1,64]{1,0:T(1,128)}, u32[]{:S(2)}) copy-start(s32[1,64]{1,0:T(1,128)} %param.9) | copy-start | bytes 772
  3.4 14.1 %copy-start.6 = (bf16[1,64,16,128]{3,2,1,0:T(8,128)(2,1)S(1)}, bf16[1,64,16,128]{3,2,1,0:T(8,128)(2,1)}, u32[]{:S(2)}) copy-start(bf16[1,64,16,128]{3,2,1,0:T(8,128)(2,1)} %param.8) | copy-start | bytes 786436
  3.4 151.5 %all-to-all-start = ((bf16[64,64,768]{2,1,0:T(8,128)(2,1)}), bf16[64,64,768]{2,1,0:T(8,128)(2,1)}, u32[]{:S(2)}, u32[]{:S(2)}) async-start(bf16[64,64,768]{2,1,0:T(8,128)(2,1)} %stack.8), calls=%async_computation | async-start | bytes 12582912 | tf_op jit(solution)/shard_map/all_to_all | solution.py:40
  158.5 6.0 copy-start.1
  159.1 5.4 copy-start.2
  159.1 5.4 collective-permute-start
  318.1 5.4 copy-start.4
  318.1 5.4 collective-permute-start.1
  476.0 0.6 copy-start.5
  476.7 5.3 collective-permute-start.2
  485.4 147.2 %all-to-all-start.3 = ((bf16[64,64,768]{2,1,0:T(8,128)(2,1)}), bf16[64,64,768]{2,1,0:T(8,128)(2,1)}, u32[]{:S(2)}, u32[]{:S(2)}) async-start(bf16[64,64,768]{2,1,0:T(8,128)(2,1)} %stack.11), calls=%async_computation.3 | async-start | bytes 12582912 | tf_op jit(solution)/shard_map/all_to_all | solution.py:40
  632.6 3.6 copy-start.3
